TPU v7x, 32 devices: a whole 2x2x4 slice. The times are simulated.
32 devices in a mesh: row: 8 (over z, y), col: 4 (over x, core).
Axes of the slice: x: 2, y: 2, z: 4, core: 2. Of those that a mesh axis runs over, the one named last changes fastest.
Arguments:
- activations: bfloat16 [512, 28672], P('col', 'row'), may hold values from -36 to 36
- output_gradient: bfloat16 [512, 8192], P('row', 'col'), may hold values from -6 to 6
- frozen_weight: bfloat16 [28672, 8192], P('row', 'col'), may hold values from -0.0390625 to 0.0390625
- sparsity_mask_pattern: int32 [7168, 8192], P('row', 'col'), may hold values from 0 to 5
- adapter_left_factor: bfloat16 [28672, 16], P('row'), may hold values from -0.19921875 to 0.19921875
- adapter_right_factor: bfloat16 [16, 8192], P(None, 'col'), may hold values from -0.359375 to 0.359375
Outputs:
- input_grad: bfloat16 [512, 28672], P('col', 'row')
- left_grad: float32 [28672, 16], P('row')
- right_grad: float32 [16, 8192], P(None, 'col')
Inputs may be any that keep to these rules, and one draw needn't show every extreme that they name: `sparsity_mask_pattern`: a pattern number of the 2:4 mask.
All inputs are finite; a program needn't handle non-finite values.
Results may differ from a plain program's by a relative error of at most 0.005.
Values may be sent and summed in bfloat16 or wider, within the bound.
No kernel may reach another device: no remote copies, remote signals or barrier semaphores. Data moves between devices by JAX's collectives and lax.ppermute only.
A program may use at most 192 MiB of HBM per device.

v0:
```python
import jax
import jax.numpy as jnp
from jax import lax
from jax.sharding import PartitionSpec as P

PAIRS = ((0, 1), (0, 2), (0, 3), (1, 2), (1, 3), (2, 3))
ADAPTER_SCALE = 2.0


def expand_mask(code):
    groups = []
    for column in range(4):
        kept = jnp.zeros(code.shape, jnp.float32)
        for pattern in range(6):
            if column in PAIRS[pattern]:
                kept = kept + (code == pattern).astype(jnp.float32)
        groups.append(kept)
    stacked = jnp.stack(groups, axis=1)
    return stacked.reshape(code.shape[0] * 4, code.shape[1])


def input_sums_of(grad_rows, merged):
    return lax.psum_scatter(
        lax.dot_general(
            grad_rows, merged, (((1,), (1,)), ((), ())), preferred_element_type=jnp.float32
        ),
        "col",
        scatter_dimension=0,
        tiled=True,
    )


def weight_grad_of(activations, grad_rows):
    return lax.dot_general(
        lax.all_gather(activations, "col", axis=0, tiled=True),
        grad_rows,
        (((0,), (0,)), ((), ())),
        preferred_element_type=jnp.float32,
    )


def per_device(
    activations,
    output_gradient,
    frozen_weight,
    sparsity_mask_pattern,
    adapter_left_factor,
    adapter_right_factor,
):
    masked = expand_mask(sparsity_mask_pattern)
    low_rank_update = jnp.dot(
        adapter_left_factor, adapter_right_factor, preferred_element_type=jnp.float32
    )
    merged = (
        masked * (frozen_weight.astype(jnp.float32) + ADAPTER_SCALE * low_rank_update)
    ).astype(jnp.bfloat16)
    grad_rows = lax.all_gather(output_gradient, "row", axis=0, tiled=True)
    all_tokens = grad_rows.shape[0]
    first_grad = weight_grad_of(activations, grad_rows)
    weight_grad, later_grads = lax.optimization_barrier((first_grad, grad_rows))
    input_grad = input_sums_of(later_grads, merged).astype(jnp.bfloat16)
    pruned_gradient = (masked * weight_grad / all_tokens).astype(jnp.bfloat16)
    left_partial = ADAPTER_SCALE * lax.dot_general(
        pruned_gradient,
        adapter_right_factor,
        (((1,), (1,)), ((), ())),
        preferred_element_type=jnp.float32,
    )
    right_partial = ADAPTER_SCALE * lax.dot_general(
        adapter_left_factor,
        pruned_gradient,
        (((0,), (0,)), ((), ())),
        preferred_element_type=jnp.float32,
    )
    right_grad = lax.psum(right_partial, "row")
    left_grad = lax.psum(left_partial, "col")
    return (input_grad, left_grad, right_grad)


def solution(mesh):
    in_specs = (
        P("col", "row"),
        P("row", "col"),
        P("row", "col"),
        P("row", "col"),
        P("row", None),
        P(None, "col"),
    )
    out_specs = (P("col", "row"), P("row", None), P(None, "col"))
    return jax.shard_map(
        per_device, mesh=mesh, in_specs=in_specs, out_specs=out_specs, check_vma=False
    )
```

profile of v0, /device:TPU:0, one launch (start us, length us, event | category | flops | bytes accessed | tf_op | source)
XLA Modules:
  0.0 334.8 jit_solution(17214782488458227821)
XLA Ops:
  7.2 0.0 copy-start
  7.2 0.0 all-gather.5.cloned.1.call-start
  7.2 0.7 all-gather.5.cloned.1.call-update
  7.9 0.0 all-gather.3.cloned.1.call-start
  8.0 0.7 all-gather.3.cloned.1.call-update
  8.7 0.0 reduce-scatter.2.cloned.1.call-start
  8.7 0.0 slice-start
  8.7 7.8 %fusion = (f32[896,1,2048]{2,0,1:T(8,128)S(1)}, pred[896,2048]{1,0:T(8,128)(4,1)S(1)}, pred[896,2048]{1,0:T(8,128)(4,1)S(1)}, pred[896,2048]{1,0:T(8,128)(4,1)}) fusion(s32[896,2048]{1,0:T(8,128)} %param.9), kind=kLoop, calls=%fused_computation.11 | loop fusion | flops 14680064 | bytes 20185088 | tf_op jit(solution)/shard_map/stack | solution.py:18
  16.5 0.0 slice-start.1
  16.6 6.5 %fusion.1 = (f32[896,1,2048]{2,0,1:T(8,128)S(1)}, pred[896,2048]{1,0:T(8,128)(4,1)S(1)}, pred[896,2048]{1,0:T(8,128)(4,1)}) fusion(pred[896,2048]{1,0:T(8,128)(4,1)S(1)} %get-tuple-element.8, s32[896,2048]{1,0:T(8,128)} %param.9), kind=kLoop, calls=%fused_computation.12 | loop fusion | flops 12845056 | bytes 20185088 | tf_op jit(solution)/shard_map/stack | solution.py:18
  23.1 0.0 slice-done
  23.1 0.0 slice-done.1
  23.1 3.6 %fusion.2 = (f32[896,1,2048]{2,0,1:T(8,128)S(1)}, pred[896,2048]{1,0:T(8,128)(4,1)}) fusion(pred[896,2048]{1,0:T(8,128)(4,1)S(1)} %get-tuple-element.12, pred[896,2048]{1,0:T(8,128)(4,1)S(1)} %get-tuple-element.9, s32[896,2048]{1,0:T(8,128)S(1)} %bitcast.20), kind=kLoop, calls=%fused_computation.13 | loop fusion | flops 11010048 | bytes 20185088 | tf_op jit(solution)/shard_map/stack | solution.py:18
  26.7 5.1 %fusion.3 = f32[896,1,2048]{2,0,1:T(8,128)S(1)} fusion(pred[896,2048]{1,0:T(8,128)(4,1)} %get-tuple-element.15, pred[896,2048]{1,0:T(8,128)(4,1)} %get-tuple-element.13, pred[896,2048]{1,0:T(8,128)(4,1)} %get-tuple-element.10), kind=kLoop, calls=%fused_computation.14 | loop fusion | flops 9175040 | bytes 12845056 | tf_op jit(solution)/shard_map/stack | solution.py:18
  31.8 10.3 %pad_maximum_fusion = f32[896,4,2048]{2,0,1:T(8,128)} fusion(f32[896,1,2048]{2,0,1:T(8,128)S(1)} %fusion.3, f32[896,1,2048]{2,0,1:T(8,128)S(1)} %get-tuple-element.14, f32[896,1,2048]{2,0,1:T(8,128)S(1)} %get-tuple-element.11, f32[896,1,2048]{2,0,1:T(8,128)S(1)} %get-tuple-element.7), kind=kLoop, calls=%fused_computation | loop fusion | flops 22020096 | bytes 58720256 | tf_op jit(solution)/shard_map/stack | solution.py:18
  42.1 33.6 %copy.9 = f32[896,4,2048]{2,1,0:T(4,128)} copy(f32[896,4,2048]{2,0,1:T(8,128)} %pad_maximum_fusion) | data formatting | bytes 58720256 | tf_op jit(solution)/shard_map/stack | solution.py:18
  75.7 33.5 %reshape.9 = f32[3584,2048]{1,0:T(8,128)} reshape(f32[896,4,2048]{2,1,0:T(4,128)} %copy.9) | data formatting | bytes 58720256 | tf_op jit(solution)/shard_map/reshape | solution.py:19
  109.2 0.0 copy-start.1
  109.2 0.0 all-gather.5.cloned.1.call-done
  109.2 0.0 copy-start.2
  109.2 0.0 all-gather.3.cloned.1.call-done
  109.2 16.2 %fusion.7 = f32[3584,2048]{1,0:T(8,128)} fusion(bf16[512,3584]{1,0:T(8,128)(2,1)} %all-gather.3.cloned.1.call-done, bf16[512,2048]{1,0:T(8,128)(2,1)} %all-gather.5.cloned.1.call-done), kind=kOutput, calls=%fused_computation.26 | convolution fusion | flops 7516192768 | bytes 35127296 | tf_op jit(solution)/shard_map/dot_general | solution.py:34
  125.4 0.0 copy-done
  125.4 0.0 copy-done.1
  125.4 0.0 copy-done.2
  125.4 21.5 %fusion.4 = f32[512,3584]{1,0:T(8,128)} fusion(bf16[512,2048]{1,0:T(8,128)(2,1)S(1)} %copy-done.2, f32[3584,2048]{1,0:T(8,128)} %reshape.9, bf16[3584,2048]{1,0:T(8,128)(2,1)} %param.8, bf16[3584,16]{0,1:T(8,128)(2,1)S(1)} %copy-done, bf16[16,2048]{1,0:T(8,128)(2,1)S(1)} %copy-done.1), kind=kOutput, calls=%fused_computation.22 | convolution fusion | flops 7787773952 | bytes 53657600 | tf_op jit(solution)/shard_map/dot_general | solution.py:24
  146.9 0.0 reduce-scatter.2.cloned.1.call-update
  147.0 0.0 all-reduce.3.cloned.1.call-start
  147.0 26.9 %multiply_convert_fusion = bf16[3584,2048]{1,0:T(8,128)(2,1)} fusion(f32[3584,2048]{1,0:T(8,128)} %reshape.9, f32[3584,2048]{1,0:T(8,128)} %fusion.7), kind=kLoop, calls=%fused_computation.1 | loop fusion | flops 22020096 | bytes 73400320 | tf_op jit(solution)/shard_map/convert_element_type | solution.py:62
  173.9 9.9 %convolution_multiply_fusion = f32[3584,16]{0,1:T(8,128)} fusion(bf16[3584,2048]{1,0:T(8,128)(2,1)} %multiply_convert_fusion, bf16[16,2048]{1,0:T(8,128)(2,1)S(1)} %copy-done.1), kind=kOutput, calls=%fused_computation.15 | convolution fusion | flops 234938368 | bytes 14974976 | tf_op jit(solution)/shard_map/dot_general | solution.py:63
  183.8 0.0 all-reduce.3.cloned.1.call-update
  183.8 0.0 all-reduce.5.cloned.1.call-start
  183.9 8.0 %fusion.5 = f32[16,2048]{1,0:T(8,128)} fusion(bf16[3584,16]{0,1:T(8,128)(2,1)S(1)} %copy-done, bf16[3584,2048]{1,0:T(8,128)(2,1)} %multiply_convert_fusion), kind=kOutput, calls=%fused_computation.24 | convolution fusion | flops 234913792 | bytes 14925824 | tf_op jit(solution)/shard_map/dot_general | solution.py:69
  191.9 0.0 all-reduce.5.cloned.1.call-update
  191.9 24.0 %reduce-scatter.2.cloned.1.call-done = f32[128,3584]{1,0:T(8,128)} async-done(((f32[512,3584]{1,0:T(8,128)}), f32[128,3584]{1,0:T(8,128)}) %reduce-scatter.2.cloned.1.call-update) | async-done | bytes 1835024 | tf_op jit(solution)/shard_map/reduce_scatter | solution.py:23
  215.9 2.5 convert_element_type.44
  218.4 32.5 %all-reduce.3.cloned.1.call-done = f32[3584,16]{0,1:T(8,128)} async-done(((f32[3584,16]{0,1:T(8,128)}), f32[3584,16]{0,1:T(8,128)}) %all-reduce.3.cloned.1.call-update) | async-done | bytes 229392 | tf_op jit(solution)/shard_map/psum | solution.py:76
  250.9 74.2 %all-reduce.5.cloned.1.call-done = f32[16,2048]{1,0:T(8,128)} async-done(((f32[16,2048]{1,0:T(8,128)}), f32[16,2048]{1,0:T(8,128)}) %all-reduce.5.cloned.1.call-update) | async-done | bytes 131088 | tf_op jit(solution)/shard_map/psum | solution.py:75
  325.0 1.6 copy.12
  326.7 1.6 copy.13
  (1 shorter events, 0.0 us)
Async XLA Ops:
  7.2 118.2 %copy-start = (bf16[3584,16]{0,1:T(8,128)(2,1)S(1)}, bf16[3584,16]{0,1:T(8,128)(2,1)}, u32[]{:S(2)}) copy-start(bf16[3584,16]{0,1:T(8,128)(2,1)} %param.10) | copy-start | bytes 344068
  7.2 102.0 %all-gather.5.cloned.1.call-start = ((), (), s32[]{:S(2)}) async-start(), calls=%async_computation.2 | async-start | bytes 2359296 | tf_op jit(solution)/shard_map/all_gather | solution.py:57
  7.9 101.3 %all-gather.3.cloned.1.call-start = ((), (), s32[]{:S(2)}) async-start(), calls=%async_computation.1 | async-start | bytes 4587520 | tf_op jit(solution)/shard_map/all_gather | solution.py:35
  8.7 207.2 %reduce-scatter.2.cloned.1.call-start = ((), (), s32[]{:S(2)}) async-start(), calls=%async_computation.3 | async-start | bytes 9175040 | tf_op jit(solution)/shard_map/reduce_scatter | solution.py:23
  8.7 14.4 %slice-start = ((s8[7340032]{0:T(1024)(128)(4,1)}), s8[4194304]{0:T(1024)(128)(4,1)S(1)}, s32[]{:S(2)}) async-start(s8[7340032]{0:T(1024)(128)(4,1)} %bitcast.19), calls=%async_computation.6 | async-start | bytes 8388608
  16.5 6.5 %slice-start.1 = ((s8[7340032]{0:T(1024)(128)(4,1)}), s8[3145728]{0:T(1024)(128)(4,1)S(1)}, s32[]{:S(2)}) async-start(s8[7340032]{0:T(1024)(128)(4,1)} %bitcast.19), calls=%async_computation.7 | async-start | bytes 6291456
  109.2 16.2 %copy-start.1 = (bf16[16,2048]{1,0:T(8,128)(2,1)S(1)}, bf16[16,2048]{1,0:T(8,128)(2,1)}, u32[]{:S(2)}) copy-start(bf16[16,2048]{1,0:T(8,128)(2,1)} %param.11) | copy-start | bytes 196612
  109.2 16.2 %copy-start.2 = (bf16[512,2048]{1,0:T(8,128)(2,1)S(1)}, bf16[512,2048]{1,0:T(8,128)(2,1)}, u32[]{:S(2)}) copy-start(bf16[512,2048]{1,0:T(8,128)(2,1)} %all-gather.5.cloned.1.call-done) | copy-start | bytes 6291460
  147.0 103.9 %all-reduce.3.cloned.1.call-start = ((), (), s32[]{:S(2)}) async-start(), calls=%async_computation.4 | async-start | bytes 458752 | tf_op jit(solution)/shard_map/psum | solution.py:76
  183.8 141.2 %all-reduce.5.cloned.1.call-start = ((), (), s32[]{:S(2)}) async-start(), calls=%async_computation.5 | async-start | bytes 262144 | tf_op jit(solution)/shard_map/psum | solution.py:75
Sparse Core Ops, SparseCore 0:
  10.1 51.8 all-gather.4
  63.5 29.9 all-gather.2
  147.1 68.7 reduce-scatter.1
  218.6 32.1 all-reduce.2
  254.6 70.3 all-reduce.4
where the time goes:
time: 336 us; the launch traced here: 335 us
  waiting for transfers between devices  132 us (39%)
  local copies, waits for them, and re-layouts  70.4 us (21%)
  other arithmetic  62.8 us (19%)
  matrix products  55.6 us (17%)
  between operations  13.8 us (4%)
    psum x1, waiting for transfers between devices, per_device(): right_grad = lax.psum(right_partial, 'row')  74.2 us
    another operation x1, local copies, waits for them, and re-layouts, expand_mask(): stacked = jnp.stack(groups, axis=1)  33.6 us
    reshape x1, local copies, waits for them, and re-layouts, expand_mask(): return stacked.reshape(code.shape[0] * 4, code.shape[1])  33.5 us
    another operation x5, other arithmetic, expand_mask(): stacked = jnp.stack(groups, axis=1)  33.3 us
    psum x1, waiting for transfers between devices, per_device(): left_grad = lax.psum(left_partial, 'col')  32.5 us
    convert_element_type x1, other arithmetic, per_device(): pruned_gradient = (masked * weight_grad / all_tokens).astype(jnp.bfloat16)  26.9 us
    reduce_scatter x1, waiting for transfers between devices, input_sums_of(): lax.psum_scatter(lax.dot_general(grad_rows, merged, (((1,), (1,)), ((), (...  24 us
    dot_general x1, matrix products, input_sums_of(): lax.dot_general(grad_rows, merged, (((1,), (1,)), ((), ())), preferred_el...  21.5 us
  transfers between devices with their start and end apart: 5, of which 3 were waited for; matrix products, arithmetic and copies ran while one was open for 44% of the time, Pallas kernels for 0%

commit v1 on v0

--- a/solution.py
+++ b/solution.py
@@ -72,7 +72,7 @@
         (((0,), (0,)), ((), ())),
         preferred_element_type=jnp.float32,
     )
-    right_grad = lax.psum(right_partial, "row")
+    right_grad = jnp.sum(lax.all_gather(right_partial, "row"), axis=0)
     left_grad = lax.psum(left_partial, "col")
     return (input_grad, left_grad, right_grad)
 

time: 336 us -> 313 us (0.932)
  waiting for transfers between devices: 132 us -> 111 us
    psum x1 -> x0, waiting for transfers between devices: 74.2 us -> none  [per_device(): right_grad = lax.psum(right_partial, 'row')]
    reduce_scatter x1, waiting for transfers between devices: 24 us -> 65.2 us  [input_sums_of(): lax.psum_scatter(lax.dot_general(grad_rows, merged, (((1,), (1,)), ((), (...]
    all_gather x0 -> x1, waiting for transfers between devices: none -> 11.5 us  [per_device(): right_grad = jnp.sum(lax.all_gather(right_partial, 'row'), axis=0)]
where the time goes in v1:
time: 313 us; the launch traced here: 312 us
  waiting for transfers between devices  111 us (35%)
  local copies, waits for them, and re-layouts  68.8 us (22%)
  other arithmetic  63 us (20%)
  matrix products  55.1 us (18%)
  between operations  13.8 us (4%)
    reduce_scatter x1, waiting for transfers between devices, input_sums_of(): lax.psum_scatter(lax.dot_general(grad_rows, merged, (((1,), (1,)), ((), (...  65.2 us
    another operation x5, other arithmetic, expand_mask(): stacked = jnp.stack(groups, axis=1)  33.8 us
    another operation x1, local copies, waits for them, and re-layouts, expand_mask(): stacked = jnp.stack(groups, axis=1)  33.6 us
    reshape x1, local copies, waits for them, and re-layouts, expand_mask(): return stacked.reshape(code.shape[0] * 4, code.shape[1])  33.5 us
    psum x1, waiting for transfers between devices, per_device(): left_grad = lax.psum(left_partial, 'col')  32.5 us
    convert_element_type x1, other arithmetic, per_device(): pruned_gradient = (masked * weight_grad / all_tokens).astype(jnp.bfloat16)  24.7 us
    dot_general x1, matrix products, input_sums_of(): lax.dot_general(grad_rows, merged, (((1,), (1,)), ((), ())), preferred_el...  21.5 us
    dot_general x1, matrix products, weight_grad_of(): lax.dot_general(lax.all_gather(activations, 'col', axis=0, tiled=True), g...  15.8 us
  transfers between devices with their start and end apart: 5, of which 3 were waited for; matrix products, arithmetic and copies ran while one was open for 44% of the time, Pallas kernels for 0%

profile of v1, /device:TPU:0, one launch (start us, length us, event | category | flops | bytes accessed | tf_op | source)
XLA Modules:
  0.0 311.7 jit_solution(6069649873027656312)
XLA Ops:
  7.2 0.0 copy-start
  7.2 0.0 all-gather.7.cloned.1.call-start
  7.2 0.7 all-gather.7.cloned.1.call-update
  7.9 0.0 all-gather.5.cloned.1.call-start
  8.0 0.7 all-gather.5.cloned.1.call-update
  8.7 0.0 all-gather.9.cloned.1.call-start
  8.7 0.0 slice-start
  8.7 7.6 %fusion = (f32[896,1,2048]{2,0,1:T(8,128)S(1)}, pred[896,2048]{1,0:T(8,128)(4,1)S(1)}, pred[896,2048]{1,0:T(8,128)(4,1)S(1)}, pred[896,2048]{1,0:T(8,128)(4,1)}) fusion(s32[896,2048]{1,0:T(8,128)} %param.9), kind=kLoop, calls=%fused_computation.11 | loop fusion | flops 14680064 | bytes 20185088 | tf_op jit(solution)/shard_map/stack | solution.py:18
  16.4 0.0 slice-start.1
  16.4 6.5 %fusion.1 = (f32[896,1,2048]{2,0,1:T(8,128)S(1)}, pred[896,2048]{1,0:T(8,128)(4,1)S(1)}, pred[896,2048]{1,0:T(8,128)(4,1)}) fusion(pred[896,2048]{1,0:T(8,128)(4,1)S(1)} %get-tuple-element.8, s32[896,2048]{1,0:T(8,128)} %param.9), kind=kLoop, calls=%fused_computation.12 | loop fusion | flops 12845056 | bytes 20185088 | tf_op jit(solution)/shard_map/stack | solution.py:18
  22.9 0.0 slice-done
  22.9 0.0 slice-done.1
  22.9 3.6 %fusion.2 = (f32[896,1,2048]{2,0,1:T(8,128)S(1)}, pred[896,2048]{1,0:T(8,128)(4,1)}) fusion(pred[896,2048]{1,0:T(8,128)(4,1)S(1)} %get-tuple-element.12, pred[896,2048]{1,0:T(8,128)(4,1)S(1)} %get-tuple-element.9, s32[896,2048]{1,0:T(8,128)S(1)} %bitcast.21), kind=kLoop, calls=%fused_computation.13 | loop fusion | flops 11010048 | bytes 20185088 | tf_op jit(solution)/shard_map/stack | solution.py:18
  26.5 5.1 %fusion.3 = f32[896,1,2048]{2,0,1:T(8,128)S(1)} fusion(pred[896,2048]{1,0:T(8,128)(4,1)} %get-tuple-element.15, pred[896,2048]{1,0:T(8,128)(4,1)} %get-tuple-element.13, pred[896,2048]{1,0:T(8,128)(4,1)} %get-tuple-element.10), kind=kLoop, calls=%fused_computation.14 | loop fusion | flops 9175040 | bytes 12845056 | tf_op jit(solution)/shard_map/stack | solution.py:18
  31.6 11.0 %pad_maximum_fusion = f32[896,4,2048]{2,0,1:T(8,128)} fusion(f32[896,1,2048]{2,0,1:T(8,128)S(1)} %fusion.3, f32[896,1,2048]{2,0,1:T(8,128)S(1)} %get-tuple-element.14, f32[896,1,2048]{2,0,1:T(8,128)S(1)} %get-tuple-element.11, f32[896,1,2048]{2,0,1:T(8,128)S(1)} %get-tuple-element.7), kind=kLoop, calls=%fused_computation | loop fusion | flops 22020096 | bytes 58720256 | tf_op jit(solution)/shard_map/stack | solution.py:18
  42.5 33.6 %copy.9 = f32[896,4,2048]{2,1,0:T(4,128)} copy(f32[896,4,2048]{2,0,1:T(8,128)} %pad_maximum_fusion) | data formatting | bytes 58720256 | tf_op jit(solution)/shard_map/stack | solution.py:18
  76.1 33.5 %reshape.9 = f32[3584,2048]{1,0:T(8,128)} reshape(f32[896,4,2048]{2,1,0:T(4,128)} %copy.9) | data formatting | bytes 58720256 | tf_op jit(solution)/shard_map/reshape | solution.py:19
  109.7 0.0 all-gather.7.cloned.1.call-done
  109.7 0.0 all-gather.5.cloned.1.call-done
  109.7 15.8 %fusion.7 = f32[3584,2048]{1,0:T(8,128)} fusion(bf16[512,3584]{1,0:T(8,128)(2,1)} %all-gather.5.cloned.1.call-done, bf16[512,2048]{1,0:T(8,128)(2,1)} %all-gather.7.cloned.1.call-done), kind=kOutput, calls=%fused_computation.26 | convolution fusion | flops 7516192768 | bytes 35127296 | tf_op jit(solution)/shard_map/dot_general | solution.py:34
  125.5 24.7 %multiply_convert_fusion = bf16[3584,2048]{1,0:T(8,128)(2,1)} fusion(f32[3584,2048]{1,0:T(8,128)} %reshape.9, f32[3584,2048]{1,0:T(8,128)} %fusion.7), kind=kLoop, calls=%fused_computation.1 | loop fusion | flops 22020096 | bytes 73400320 | tf_op jit(solution)/shard_map/convert_element_type | solution.py:62
  150.2 0.0 copy-done
  150.2 0.0 copy-start.1
  150.2 0.0 copy-start.2
  150.2 8.0 %fusion.5 = f32[16,2048]{1,0:T(8,128)} fusion(bf16[3584,16]{0,1:T(8,128)(2,1)S(1)} %copy-done, bf16[3584,2048]{1,0:T(8,128)(2,1)} %multiply_convert_fusion), kind=kOutput, calls=%fused_computation.24 | convolution fusion | flops 234913792 | bytes 14925824 | tf_op jit(solution)/shard_map/dot_general | solution.py:69
  158.2 0.0 all-gather.9.cloned.1.call-update
  158.2 0.0 reduce-scatter.2.cloned.1.call-start
  158.3 0.0 copy-done.1
  158.3 0.0 copy-done.2
  158.3 21.5 %fusion.4 = f32[512,3584]{1,0:T(8,128)} fusion(bf16[512,2048]{1,0:T(8,128)(2,1)S(1)} %copy-done.2, f32[3584,2048]{1,0:T(8,128)} %reshape.9, bf16[3584,2048]{1,0:T(8,128)(2,1)} %param.8, bf16[3584,16]{0,1:T(8,128)(2,1)S(1)} %copy-done, bf16[16,2048]{1,0:T(8,128)(2,1)S(1)} %copy-done.1), kind=kOutput, calls=%fused_computation.22 | convolution fusion | flops 7787773952 | bytes 53657600 | tf_op jit(solution)/shard_map/dot_general | solution.py:24
  179.8 0.0 reduce-scatter.2.cloned.1.call-update
  179.8 0.3 all-reduce.2.cloned.1.call-start
  180.1 9.8 %convolution_multiply_fusion = f32[3584,16]{0,1:T(8,128)} fusion(bf16[3584,2048]{1,0:T(8,128)(2,1)} %multiply_convert_fusion, bf16[16,2048]{1,0:T(8,128)(2,1)S(1)} %copy-done.1), kind=kOutput, calls=%fused_computation.15 | convolution fusion | flops 234938368 | bytes 14974976 | tf_op jit(solution)/shard_map/dot_general | solution.py:63
  189.8 0.0 all-reduce.2.cloned.1.call-update
  189.9 11.5 %all-gather.9.cloned.1.call-done = f32[128,2048]{1,0:T(8,128)} async-done(((f32[16,2048]{1,0:T(8,128)}), f32[128,2048]{1,0:T(8,128)}) %all-gather.9.cloned.1.call-update) | async-done | bytes 1048592 | tf_op jit(solution)/shard_map/all_gather | solution.py:75
  201.4 1.9 reduce_sum.9
  203.4 65.2 %reduce-scatter.2.cloned.1.call-done = f32[128,3584]{1,0:T(8,128)} async-done(((f32[512,3584]{1,0:T(8,128)}), f32[128,3584]{1,0:T(8,128)}) %reduce-scatter.2.cloned.1.call-update) | async-done | bytes 1835024 | tf_op jit(solution)/shard_map/reduce_scatter | solution.py:23
  268.5 2.5 convert_element_type.44
  271.0 32.5 %all-reduce.2.cloned.1.call-done = f32[3584,16]{0,1:T(8,128)} async-done(((f32[3584,16]{0,1:T(8,128)}), f32[3584,16]{0,1:T(8,128)}) %all-reduce.2.cloned.1.call-update) | async-done | bytes 229392 | tf_op jit(solution)/shard_map/psum | solution.py:76
  303.5 1.6 copy.11
  (1 shorter events, 0.0 us)
Async XLA Ops:
  7.2 143.0 %copy-start = (bf16[3584,16]{0,1:T(8,128)(2,1)S(1)}, bf16[3584,16]{0,1:T(8,128)(2,1)}, u32[]{:S(2)}) copy-start(bf16[3584,16]{0,1:T(8,128)(2,1)} %param.10) | copy-start | bytes 344068
  7.2 102.5 %all-gather.7.cloned.1.call-start = ((), (), s32[]{:S(2)}) async-start(), calls=%async_computation.2 | async-start | bytes 2359296 | tf_op jit(solution)/shard_map/all_gather | solution.py:57
  7.9 101.7 %all-gather.5.cloned.1.call-start = ((), (), s32[]{:S(2)}) async-start(), calls=%async_computation.1 | async-start | bytes 4587520 | tf_op jit(solution)/shard_map/all_gather | solution.py:35
  8.7 192.7 %all-gather.9.cloned.1.call-start = ((), (), s32[]{:S(2)}) async-start(), calls=%async_computation.5 | async-start | bytes 1179648 | tf_op jit(solution)/shard_map/all_gather | solution.py:75
  8.7 14.2 %slice-start = ((s8[7340032]{0:T(1024)(128)(4,1)}), s8[4194304]{0:T(1024)(128)(4,1)S(1)}, s32[]{:S(2)}) async-start(s8[7340032]{0:T(1024)(128)(4,1)} %bitcast.20), calls=%async_computation.6 | async-start | bytes 8388608
  16.4 6.5 %slice-start.1 = ((s8[7340032]{0:T(1024)(128)(4,1)}), s8[3145728]{0:T(1024)(128)(4,1)S(1)}, s32[]{:S(2)}) async-start(s8[7340032]{0:T(1024)(128)(4,1)} %bitcast.20), calls=%async_computation.7 | async-start | bytes 6291456
  150.2 8.1 %copy-start.1 = (bf16[16,2048]{1,0:T(8,128)(2,1)S(1)}, bf16[16,2048]{1,0:T(8,128)(2,1)}, u32[]{:S(2)}) copy-start(bf16[16,2048]{1,0:T(8,128)(2,1)} %param.11) | copy-start | bytes 196612
  150.2 8.1 %copy-start.2 = (bf16[512,2048]{1,0:T(8,128)(2,1)S(1)}, bf16[512,2048]{1,0:T(8,128)(2,1)}, u32[]{:S(2)}) copy-start(bf16[512,2048]{1,0:T(8,128)(2,1)} %all-gather.7.cloned.1.call-done) | copy-start | bytes 6291460
  158.2 110.3 %reduce-scatter.2.cloned.1.call-start = ((), (), s32[]{:S(2)}) async-start(), calls=%async_computation.3 | async-start | bytes 9175040 | tf_op jit(solution)/shard_map/reduce_scatter | solution.py:23
  179.8 123.7 %all-reduce.2.cloned.1.call-start = ((), (), s32[]{:S(2)}) async-start(), calls=%async_computation.4 | async-start | bytes 458752 | tf_op jit(solution)/shard_map/psum | solution.py:76
Sparse Core Ops, SparseCore 0:
  10.1 51.7 all-gather.6
  63.5 29.9 all-gather.4
  158.3 43.0 all-gather.8
  203.8 64.6 reduce-scatter.1
  271.3 32.1 all-reduce.1
